TPU v7x, 256 devices: a whole 4x4x8 slice. The times are simulated.
256 devices in a mesh: samples: 32 (over y, x, core), cols: 8 (over z).
Axes of the slice: x: 4, y: 4, z: 8, core: 2. Of those that a mesh axis runs over, the one named last changes fastest.
Arguments:
- features: bfloat16 [131072, 440], P('samples'), may hold values from -6 to 6
- labels: int32 [131072], P('samples'), may hold values from 0 to 146
- weights: float32 [131072, 147], P('samples'), may hold values from -6 to 6
- block_order: int32 [32], replicated, may hold values from 0 to 31, each once
- block_starts: int32 [32], replicated, may hold values from 0 to 3968
- inverses: float32 [4, 4096, 4096], P(None, 'samples', 'cols'), may hold values from -0.125 to 1.5
Outputs:
- new_weights: float32 [131072, 147], P('samples')
All inputs are finite; a program needn't handle non-finite values.
Results may differ from a plain program's by a relative error of at most 0.0005.
Values may be sent and summed in bfloat16 or wider, within the bound.
A program may use at most 128 MiB of HBM per device.

v0:
```python
import math

import jax
import jax.numpy as jnp
from jax import lax
from jax.experimental import pallas as pl
from jax.experimental.pallas import tpu as pltpu
from jax.sharding import Mesh
from jax.sharding import PartitionSpec as P

SAMPLES = ("sy", "sx", "sc")
MESH = pl.DeviceIdType.MESH
HIGHEST = lax.Precision.HIGHEST
RIDGE = 0.5
UPD = 4
BLOCKS = 32
CHIPS = 16
COLS = 8
SPAN = 128
PIECE = 16
GROUP = 512
WIDTH = 440
DEPTH = 512
LANES = 128
CLASSES = 147
ROWS = 4096
NBLOCK = 1024
WINDOW = 256
EARLIER = [(early, late) for late in range(UPD) for early in range(late)]
VMEM = pl.BlockSpec(memory_space=pltpu.VMEM)
SMEM = pl.BlockSpec(memory_space=pltpu.SMEM)
ANY = pl.BlockSpec(memory_space=pl.ANY)
F32, BF16 = jnp.float32, jnp.bfloat16
NT = (((1,), (1,)), ((), ()))


def push(src, dst, send, recv, device):
    pltpu.make_async_remote_copy(
        src_ref=src,
        dst_ref=dst,
        send_sem=send,
        recv_sem=recv,
        device_id=device,
        device_id_type=MESH,
    ).start()


def drain(ref, sem):
    pltpu.make_async_copy(ref, ref, sem).wait()


def over(low, high, body):
    def step(index, carry):
        body(index)
        return carry

    lax.fori_loop(low, high, step, 0)


def iota(shape, dim):
    return lax.broadcasted_iota(jnp.int32, shape, dim)


def dot(a, b):
    return jnp.dot(a, b, preferred_element_type=F32)


def split3(value):
    high = value.astype(BF16).astype(F32)
    rest = value - high
    middle = rest.astype(BF16).astype(F32)
    return high, middle, rest - middle


def kernel_values(exponent):
    return jnp.exp2(exponent * (math.log2(math.e) / WIDTH)).astype(BF16)


def window_of(start):
    base = jnp.minimum(start // LANES, (ROWS - WINDOW) // LANES) * LANES
    return pl.multiple_of(base, LANES), start - base


MEM, MEM_REST, SIB, SIB_REST, TERM, FB, INV, SP, SPR, SR, SD, SH, SX, SC = (
    0, 1, 2, 3, 4, 5, 6, 7, 8, 10, 14, 18, 22, 26,
)
N_SEM = 30


def main_kernel(
    ft, wt, labels, inv, order, block_starts, out,
    fa, wv, wn, wide, picks, iv, a, mem, fb, o, term_send, acc, p, m,
    got_p, r0, r_send, r_full, d_part, d_got, d_own, h_own, h_full, c_part, c_got, high, low,
    send, recv, load,
):
    y = lax.axis_index("sy")
    x = lax.axis_index("sx")
    c = lax.axis_index("sc")
    z = lax.axis_index("cols")
    chip = y * 4 + x
    shard = chip * 2 + c
    sib = (y, x, 1 - c, z)
    scale = 1.0 / math.sqrt(ROWS * 32)

    def peer(offset):
        row = lax.rem(y + offset // 4, 4)
        col = lax.rem(x + lax.rem(offset, 4), 4)
        return row, col, row * 4 + col

    loads = [
        pltpu.make_async_copy(ft, fa.at[pl.ds(0, WIDTH)], load.at[0]),
        pltpu.make_async_copy(wt, wv, load.at[1]),
        pltpu.make_async_copy(inv, iv.at[c], load.at[2]),
    ]
    for copy in loads:
        copy.start()

    barrier = pltpu.get_barrier_semaphore()

    def greet_plane(offset):
        row, col, _ = peer(offset)
        for core in range(2):

            @pl.when((offset > 0) | (core != c))
            def _():
                pl.semaphore_signal(
                    barrier, inc=1, device_id=(row, col, core, z), device_id_type=MESH
                )

    def greet_column(offset):
        for core in range(2):
            pl.semaphore_signal(
                barrier, inc=1, device_id=(y, x, core, lax.rem(z + offset, COLS)), device_id_type=MESH
            )

    over(0, CHIPS, greet_plane)
    over(1, COLS, greet_column)

    starts = []
    for t in range(UPD):
        start = jnp.int32(0)
        for block in range(BLOCKS):
            start += jnp.where(order[t] == block, block_starts[block], 0)
        starts.append(start)

    column = iota((1, LANES), 1)
    target = jnp.full((1, LANES), -1, jnp.int32)
    for t in range(UPD):
        here = column // PIECE == t
        target = jnp.where(here, starts[t] + z * PIECE + lax.rem(column, PIECE), target)
    picks[...] = (iota((ROWS, LANES), 0) == target).astype(BF16)
    loads[0].wait()
    chosen = dot(fa[0:WIDTH, :], picks[...])
    norm = jnp.sum(jnp.square(chosen), axis=0, keepdims=True)
    line = iota((8, LANES), 0)
    extra = jnp.where(line < 6, 1.0, 0.0)
    for number, part in enumerate(split3(norm)):
        extra = jnp.where(line == number + 3, -part, extra)
    rest = jnp.zeros((DEPTH - WIDTH - 8, LANES), F32)
    chosen = jnp.concatenate([2.0 * chosen, extra, rest], axis=0).T.astype(BF16)
    for t in range(UPD):
        mem[t] = chosen[t * PIECE : (t + 1) * PIECE]

    pl.semaphore_wait(barrier, 31 + 14)

    def send_members(first, count, number):
        def body(offset):
            row, col, _ = peer(offset)
            push(
                mem.at[pl.ds(first, count)],
                a.at[pl.ds(first, count), chip, c],
                send.at[number],
                recv.at[number],
                (row, col, c, z),
            )

        over(1, CHIPS, body)
        for t in range(first, first + count):
            a[t, chip, c] = mem[t]

    def forward_members(first, count, number, onward):
        drain(a.at[pl.ds(first, count), pl.ds(0, 15), 0], recv.at[number])
        ours = a.at[pl.ds(first, count), :, c]
        push(ours, ours, send.at[onward], recv.at[onward], sib)

    send_members(0, 1, MEM)
    send_members(1, 3, MEM_REST)

    line = iota((8, NBLOCK), 0)
    for block in range(ROWS // NBLOCK):
        cols = pl.ds(block * NBLOCK, NBLOCK)
        norm = jnp.sum(jnp.square(fa[0:WIDTH, cols].astype(F32)), axis=0, keepdims=True)
        extra = jnp.where(line < 6, 1.0, 0.0)
        for number, part in enumerate(split3(norm)):
            extra = jnp.where(line == number, -part, extra)
        tail = fa[432:440, cols].astype(F32)
        fa[432:448, cols] = jnp.concatenate([tail, extra], axis=0).astype(BF16)
        fa[448:DEPTH, cols] = jnp.zeros((DEPTH - 448, NBLOCK), BF16)

    loads[1].wait()
    values = [dot(part.astype(BF16), picks[...]) for part in split3(wv[...])]
    values = values[0] + values[1] + values[2]
    known = dot(jnp.broadcast_to(labels[...].astype(F32), (8, ROWS)).astype(BF16), picks[...])
    onehot = (iota((CLASSES, LANES), 0).astype(F32) == known[0:1]).astype(F32)
    wide[...] = jnp.zeros_like(wide)
    wide[0:CLASSES, :] = onehot - RIDGE * values
    terms = wide[...].T
    for t in range(UPD):
        first = terms[t * PIECE : (t + 1) * PIECE, 0:LANES]
        second = terms[t * PIECE : (t + 1) * PIECE, LANES:]
        o[t, c] = jnp.where(c == 0, first, second)
        term_send[t] = jnp.where(c == 0, second, first)
    push(term_send, o.at[:, c], send.at[TERM], recv.at[TERM], sib)
    for t in range(UPD - 1):
        picks[...] = (iota((ROWS, SPAN), 0) == starts[t] + iota((1, SPAN), 1)).astype(BF16)
        fb[c, t] = dot(fa[...], picks[...]).astype(BF16)
    push(fb.at[c], fb.at[c], send.at[FB], recv.at[FB], sib)
    push(inv, iv.at[c], send.at[INV], recv.at[INV], sib)
    for block in range(ROWS // NBLOCK):
        cols = pl.ds(block * NBLOCK, NBLOCK)
        wn[cols, :] = jnp.zeros((NBLOCK, 2 * LANES), BF16)
        wn[cols, 0:CLASSES] = wv[:, cols].T.astype(BF16)

    def panel(t, first, last):
        def body(block):
            cols = pl.ds(pl.multiple_of(block * NBLOCK, NBLOCK), NBLOCK)
            for half in range(2):
                rows = pl.ds(half * 256, 256)
                lines = a[t, pl.ds(half * 8, 8)].reshape(256, DEPTH)
                values = kernel_values(dot(lines, fa[:, cols]))
                acc[rows, :] += dot(values, wn[cols, :])

        if first == 0:
            acc[...] = jnp.zeros_like(acc)
        over(first, last, body)
        if last == ROWS // NBLOCK:
            for half in range(2):
                part = acc[:, half * LANES : (half + 1) * LANES].astype(BF16)
                p[half, t] = part.reshape(CHIPS, 32, LANES)

    def margin(early, late):
        lines = a[late].reshape(GROUP, DEPTH)
        for half in range(2):
            m[EARLIER.index((early, late)), half] = kernel_values(dot(lines, fb[half, early]))

    def send_products(first, count, number):
        def body(offset):
            row, col, other = peer(offset)
            for core in range(2):

                @pl.when((offset > 0) | (core != c))
                def _():
                    push(
                        p.at[core, pl.ds(first, count), other],
                        got_p.at[pl.ds(first, count), shard],
                        send.at[number],
                        recv.at[number],
                        (row, col, core, z),
                    )

        over(0, CHIPS, body)

    def sums_of_products(first, count, number):
        drain(got_p.at[pl.ds(first, count), pl.ds(0, 31)], recv.at[number])
        for t in range(first, first + count):
            got_p[t, shard] = p[c, t, chip]
            own = o[t].reshape(32, LANES)
            r0[t] = own - scale * jnp.sum(got_p[t].astype(F32), axis=0)

    def send_residual(t):
        def body(offset):
            row, col, _ = peer(offset)
            push(r_send.at[t], r_full.at[t, chip], send.at[SR + t], recv.at[SR + t], (row, col, c, z))

        over(1, CHIPS, body)
        r_full[t, chip] = r_send[t]

    def split_inverse(t):
        for half in range(2):
            value = iv[half, t]
            top = value.astype(BF16)
            high[t, half] = top
            low[t, half] = (value - top.astype(F32)).astype(BF16)

    def partial_delta(t):
        drain(r_full.at[t, pl.ds(0, 15)], recv.at[SR + t])
        residual = r_full[t].reshape(GROUP, LANES)
        top = residual.astype(BF16)
        rest = (residual - top.astype(F32)).astype(BF16)
        for half in range(2):
            value = dot(high[t, half], top) + dot(high[t, half], rest) + dot(low[t, half], top)
            d_part[t, pl.ds(half * 4, 4)] = value.reshape(4, 32, LANES)

        def body(offset):
            other = lax.rem(z + offset, COLS)
            push(d_part.at[t, other], d_got.at[t, z], send.at[SD + t], recv.at[SD + t], (y, x, c, other))

        over(1, COLS, body)
        d_got[t, z] = d_part[t, z]

    keeper = z // 4
    place = pl.ds(pl.multiple_of(lax.rem(z, 4) * 32, 32), 32)

    def finish_delta(t):
        drain(d_got.at[t, pl.ds(0, 7)], recv.at[SD + t])
        delta = jnp.sum(d_got[t], axis=0)
        d_own[t] = delta
        if t < UPD - 1:
            h_own[t] = delta.astype(BF16)

            def send_high(offset):
                other = lax.rem(z + offset, COLS)
                push(h_own.at[t], h_full.at[t, z], send.at[SH + t], recv.at[SH + t], (y, x, c, other))

            over(1, COLS, send_high)
            h_full[t, z] = h_own[t]

        def send_result(offset):
            other = lax.rem(z + offset, COLS)

            @pl.when((offset > 0) | (keeper != c))
            def _():
                push(
                    d_own.at[t], out.at[t, c, place], send.at[SX + t], recv.at[SX + t],
                    (y, x, keeper, other),
                )

        over(0, COLS, send_result)

        @pl.when(keeper == c)
        def _():
            out[t, c, place] = d_own[t]

    def corrections(early, late):
        total = None
        for half in range(2):
            lines = h_full[early, pl.ds(half * 4, 4)].reshape(SPAN, LANES)
            part = dot(m[EARLIER.index((early, late)), half], lines)
            total = part if total is None else total + part
        return total

    def next_residual(t, partial):
        late = t + 1
        drain(h_full.at[t, pl.ds(0, 7)], recv.at[SH + t])
        part = corrections(t, late)
        partial = part if partial is None else partial + part
        c_part[t] = partial.astype(BF16).reshape(CHIPS, 32, LANES)

        def body(offset):
            row, col, other = peer(offset)
            push(
                c_part.at[t, other], c_got.at[t, chip], send.at[SC + t], recv.at[SC + t], (row, col, c, z)
            )

        over(1, CHIPS, body)
        c_got[t, chip] = c_part[t, chip]
        line = iota((32, 2 * SPAN), 0)
        column = iota((32, 2 * SPAN), 1)
        member = starts[late] + z * PIECE + lax.rem(line, PIECE)
        same = line // PIECE == column // SPAN
        shared = jnp.zeros((32, LANES), F32)
        for early in range(late):
            hit = same & (member == starts[early] + lax.rem(column, SPAN))
            shared += dot(
                jnp.where(hit, RIDGE, 0.0).astype(BF16), h_full[early].reshape(2 * SPAN, LANES)
            )
        drain(c_got.at[t, pl.ds(0, 15)], recv.at[SC + t])
        r_send[late] = r0[late] - shared - scale * jnp.sum(c_got[t].astype(F32), axis=0)
        send_residual(late)

    whole = ROWS // NBLOCK
    forward_members(0, 1, MEM, SIB)
    loads[2].wait()
    drain(a.at[pl.ds(0, 1), :, 1 - c], recv.at[SIB])
    panel(0, 0, whole // 2)
    forward_members(1, 3, MEM_REST, SIB_REST)
    panel(0, whole // 2, whole)
    send_products(0, 1, SP)
    drain(fb.at[1 - c], recv.at[FB])
    drain(iv.at[1 - c], recv.at[INV])
    drain(o.at[:, 1 - c], recv.at[TERM])
    drain(a.at[pl.ds(1, 3), :, 1 - c], recv.at[SIB_REST])
    split_inverse(0)
    panel(1, 0, whole)
    sums_of_products(0, 1, SP)
    r_send[0] = r0[0]
    send_residual(0)
    panel(2, 0, whole)
    partial_delta(0)
    send_products(1, 2, SPR)
    panel(3, 0, whole)
    finish_delta(0)
    send_products(3, 1, SPR + 1)
    margin(0, 1)
    next_residual_ready = None
    sums_of_products(1, 2, SPR)
    next_residual(0, next_residual_ready)
    for pair in ((0, 2), (1, 2)):
        margin(*pair)
    split_inverse(1)
    partial_delta(1)
    for pair in ((0, 3), (1, 3)):
        margin(*pair)
    finish_delta(1)
    sums_of_products(3, 1, SPR + 1)
    next_residual(1, corrections(0, 2))
    split_inverse(2)
    margin(2, 3)
    partial_delta(2)
    partial = corrections(0, 3) + corrections(1, 3)
    finish_delta(2)
    split_inverse(3)
    next_residual(2, partial)
    partial_delta(3)
    finish_delta(3)

    for t in range(UPD):

        @pl.when(keeper == c)
        def _():
            drain(d_got.at[t, pl.ds(0, 7)], recv.at[SX + t])
            drain(d_got.at[t, pl.ds(0, 7)], send.at[SX + t])

        @pl.when(keeper != c)
        def _():
            drain(d_got.at[t], recv.at[SX + t])
            drain(d_got.at[t], send.at[SX + t])

        drain(r_full.at[t, pl.ds(0, 15)], send.at[SR + t])
        drain(d_got.at[t, pl.ds(0, 7)], send.at[SD + t])
        if t < UPD - 1:
            drain(h_full.at[t, pl.ds(0, 7)], send.at[SH + t])
            drain(c_got.at[t, pl.ds(0, 15)], send.at[SC + t])
    drain(got_p.at[pl.ds(0, 1), pl.ds(0, 31)], send.at[SP])
    drain(got_p.at[pl.ds(0, 2), pl.ds(0, 31)], send.at[SPR])
    drain(got_p.at[pl.ds(0, 1), pl.ds(0, 31)], send.at[SPR + 1])
    drain(a.at[pl.ds(0, 1), pl.ds(0, 15), 0], send.at[MEM])
    drain(a.at[pl.ds(1, 3), pl.ds(0, 15), 0], send.at[MEM_REST])
    drain(a.at[pl.ds(0, 1), :, 0], send.at[SIB])
    drain(a.at[pl.ds(1, 3), :, 0], send.at[SIB_REST])
    drain(fb.at[0], send.at[FB])
    drain(iv.at[0], send.at[INV])
    drain(term_send, send.at[TERM])


def deltas_of(ft, wt, labels, inv, order, starts):
    vmem = pltpu.VMEM
    return pl.pallas_call(
        main_kernel,
        out_shape=jax.ShapeDtypeStruct((UPD, 2, SPAN, LANES), F32),
        in_specs=[ANY, ANY, VMEM, ANY, SMEM, SMEM],
        out_specs=VMEM,
        scratch_shapes=[
            vmem((DEPTH, ROWS), BF16),
            vmem((CLASSES, ROWS), F32),
            vmem((ROWS, 2 * LANES), BF16),
            vmem((2 * LANES, LANES), F32),
            vmem((ROWS, LANES), BF16),
            vmem((2, UPD, SPAN, GROUP), F32),
            vmem((UPD, CHIPS, 2, PIECE, DEPTH), BF16),
            vmem((UPD, PIECE, DEPTH), BF16),
            vmem((2, UPD - 1, DEPTH, SPAN), BF16),
            vmem((UPD, 2, PIECE, LANES), F32),
            vmem((UPD, PIECE, LANES), F32),
            vmem((GROUP, 2 * LANES), F32),
            vmem((2, UPD, CHIPS, 32, LANES), BF16),
            vmem((len(EARLIER), 2, GROUP, SPAN), BF16),
            vmem((UPD, 2 * CHIPS, 32, LANES), BF16),
            vmem((UPD, 32, LANES), F32),
            vmem((UPD, 32, LANES), F32),
            vmem((UPD, CHIPS, 32, LANES), F32),
            vmem((UPD, COLS, 32, LANES), F32),
            vmem((UPD, COLS, 32, LANES), F32),
            vmem((UPD, 32, LANES), F32),
            vmem((UPD - 1, 32, LANES), BF16),
            vmem((UPD - 1, COLS, 32, LANES), BF16),
            vmem((UPD - 1, CHIPS, 32, LANES), BF16),
            vmem((UPD - 1, CHIPS, 32, LANES), BF16),
            vmem((UPD, 2, SPAN, GROUP), BF16),
            vmem((UPD, 2, SPAN, GROUP), BF16),
            pltpu.SemaphoreType.DMA((N_SEM,)),
            pltpu.SemaphoreType.DMA((N_SEM,)),
            pltpu.SemaphoreType.DMA((3,)),
        ],
        compiler_params=pltpu.CompilerParams(
            collective_id=0, has_side_effects=True, vmem_limit_bytes=48 << 20
        ),
        name="updates",
    )(ft, wt, labels, inv, order, starts)


def add_kernel(wt, deltas, order, block_starts, out):
    out[...] = wt[...]
    for t in range(UPD):
        base, shift = window_of(block_starts[order[t]])
        rows = jnp.concatenate([deltas[t, 0].T, deltas[t, 1].T], axis=0)[:CLASSES]
        wide = jnp.concatenate([rows, jnp.zeros((CLASSES, WINDOW - SPAN), F32)], axis=1)
        out[:, pl.ds(base, WINDOW)] += pltpu.roll(wide, shift, 1)


def add_deltas(wt, deltas, order, starts):
    return pl.pallas_call(
        add_kernel,
        out_shape=jax.ShapeDtypeStruct(wt.shape, wt.dtype),
        in_specs=[VMEM, VMEM, SMEM, SMEM],
        out_specs=VMEM,
        compiler_params=pltpu.CompilerParams(vmem_limit_bytes=16 << 20),
        name="add_deltas",
    )(wt, deltas, order, starts)


def local(features, labels, weights, block_order, block_starts, inverses):
    wt = weights.T
    deltas = deltas_of(
        features.T, wt, labels.reshape(1, ROWS), inverses, block_order, block_starts
    )
    return add_deltas(wt, deltas, block_order, block_starts).T


def solution(mesh):
    finer = Mesh(
        mesh.devices.reshape(4, 4, 2, mesh.shape["cols"]), ("sy", "sx", "sc", "cols")
    )
    in_specs = (P(SAMPLES, None), P(SAMPLES), P(SAMPLES, None), P(), P(), P(None, SAMPLES, "cols"))
    return jax.shard_map(
        local, mesh=finer, in_specs=in_specs, out_specs=P(SAMPLES, None), check_vma=False
    )
```

profile of v0, /device:TPU:1, one launch (start us, length us, event | category | flops | bytes accessed | tf_op | source)
XLA Modules:
  0.0 130.5 jit_solution(8995698963917296341)
XLA Ops:
  0.0 0.0 copy-start
  0.0 1.7 %copy-done = f32[4096,147]{0,1:T(8,128)S(1)} copy-done((f32[4096,147]{0,1:T(8,128)S(1)}, f32[4096,147]{0,1:T(8,128)}, u32[]{:S(2)}) %copy-start) | copy-done | bytes 2408472
  1.7 0.0 copy-start.1
  1.7 1.2 copy-done.1
  2.9 0.0 copy-start.2
  2.9 0.7 copy-done.2
  3.6 0.0 copy-start.3
  3.6 0.7 copy-done.3
  4.3 0.0 copy-start.4
  4.3 0.7 copy-done.4
  5.0 123.2 %updates.1.deltas = f32[4,2,128,128]{3,2,1,0:T(8,128)S(1)} custom-call(bf16[440,4096]{1,0:T(8,128)(2,1)} %bitcast.7, f32[147,4096]{1,0:T(8,128)S(1)} %bitcast.4, s32[1,4096]{1,0:T(1,128)S(1)} %bitcast.6, f32[4,128,512]{2,1,0:T(8,128)S(1)} %copy-done.1, s32[32]{0:T(128)S(1)} %copy-done.3, s32[32]{0:T(128)S(1)} %copy-done.4), custom_call_target="tpu_custom_call" | custom-call | tf_op jit(solution)/shard_map/updates/pallas_call | solution.py:448
  128.2 2.4 %add_deltas.1 = f32[147,4096]{1,0:T(8,128)} custom-call(f32[147,4096]{1,0:T(8,128)S(1)} %bitcast.5, f32[4,2,128,128]{3,2,1,0:T(8,128)S(1)} %updates.1.deltas, s32[32]{0:T(128)S(1)} %copy-done.3, s32[32]{0:T(128)S(1)} %copy-done.4), custom_call_target="tpu_custom_call" | custom-call | tf_op jit(solution)/shard_map/add_deltas/pallas_call | solution.py:502
Async XLA Ops:
  0.0 1.7 %copy-start = (f32[4096,147]{0,1:T(8,128)S(1)}, f32[4096,147]{0,1:T(8,128)}, u32[]{:S(2)}) copy-start(f32[4096,147]{0,1:T(8,128)} %param.8) | copy-start | bytes 7225348
  1.7 1.2 copy-start.1
  2.9 0.7 copy-start.2
  3.6 0.7 copy-start.3
  4.3 0.7 copy-start.4
where the time goes:
time: 131 us
  Pallas kernels  126 us (96%)
  local copies, waits for them, and re-layouts  4.95 us (4%)
    pallas_call x1, Pallas kernels, deltas_of(): pl.pallas_call(main_kernel, out_shape=jax.ShapeDtypeStruct((UPD, 2, SPAN,...  123 us
    unnamed x10, local copies, waits for them, and re-layouts  4.95 us

commit v1 on v0

--- a/solution.py
+++ b/solution.py
@@ -29,7 +29,7 @@
 EARLIER = [(early, late) for late in range(UPD) for early in range(late)]
 VMEM = pl.BlockSpec(memory_space=pltpu.VMEM)
 SMEM = pl.BlockSpec(memory_space=pltpu.SMEM)
-ANY = pl.BlockSpec(memory_space=pl.ANY)
+ANY = pl.BlockSpec(memory_space=pltpu.HBM)
 F32, BF16 = jnp.float32, jnp.bfloat16
 NT = (((1,), (1,)), ((), ()))
 
@@ -339,7 +339,7 @@
             total = part if total is None else total + part
         return total
 
-    def next_residual(t, partial):
+    def send_correction(t, partial):
         late = t + 1
         drain(h_full.at[t, pl.ds(0, 7)], recv.at[SH + t])
         part = corrections(t, late)
@@ -354,6 +354,9 @@
 
         over(1, CHIPS, body)
         c_got[t, chip] = c_part[t, chip]
+
+    def next_residual(t):
+        late = t + 1
         line = iota((32, 2 * SPAN), 0)
         column = iota((32, 2 * SPAN), 1)
         member = starts[late] + z * PIECE + lax.rem(line, PIECE)
@@ -392,25 +395,28 @@
     finish_delta(0)
     send_products(3, 1, SPR + 1)
     margin(0, 1)
-    next_residual_ready = None
+    send_correction(0, None)
     sums_of_products(1, 2, SPR)
-    next_residual(0, next_residual_ready)
-    for pair in ((0, 2), (1, 2)):
-        margin(*pair)
+    next_residual(0)
     split_inverse(1)
     partial_delta(1)
-    for pair in ((0, 3), (1, 3)):
-        margin(*pair)
+    margin(0, 2)
+    margin(0, 3)
+    partial = corrections(0, 2)
     finish_delta(1)
+    margin(1, 2)
+    margin(1, 3)
+    send_correction(1, partial)
     sums_of_products(3, 1, SPR + 1)
-    next_residual(1, corrections(0, 2))
+    next_residual(1)
     split_inverse(2)
-    margin(2, 3)
     partial_delta(2)
     partial = corrections(0, 3) + corrections(1, 3)
     finish_delta(2)
+    margin(2, 3)
+    send_correction(2, partial)
     split_inverse(3)
-    next_residual(2, partial)
+    next_residual(2)
     partial_delta(3)
     finish_delta(3)
 
@@ -483,7 +489,7 @@
             pltpu.SemaphoreType.DMA((3,)),
         ],
         compiler_params=pltpu.CompilerParams(
-            collective_id=0, has_side_effects=True, vmem_limit_bytes=48 << 20
+            collective_id=0, has_side_effects=True, vmem_limit_bytes=64 << 20
         ),
         name="updates",
     )(ft, wt, labels, inv, order, starts)
@@ -504,7 +510,7 @@
         out_shape=jax.ShapeDtypeStruct(wt.shape, wt.dtype),
         in_specs=[VMEM, VMEM, SMEM, SMEM],
         out_specs=VMEM,
-        compiler_params=pltpu.CompilerParams(vmem_limit_bytes=16 << 20),
+        compiler_params=pltpu.CompilerParams(vmem_limit_bytes=64 << 20),
         name="add_deltas",
     )(wt, deltas, order, starts)
 

time: 131 us -> 128 us (0.977)
  local copies, waits for them, and re-layouts: 4.95 us -> 0 us
  Pallas kernels: 126 us -> 128 us
    unnamed x10 -> x0, local copies, waits for them, and re-layouts: 4.95 us -> none
where the time goes in v1:
time: 128 us
  Pallas kernels  128 us (100%)
    pallas_call x1, Pallas kernels, deltas_of(): pl.pallas_call(main_kernel, out_shape=jax.ShapeDtypeStruct((UPD, 2, SPAN,...  124 us
    pallas_call x1, Pallas kernels, add_deltas(): pl.pallas_call(add_kernel, out_shape=jax.ShapeDtypeStruct(wt.shape, wt.dt...  3.64 us

profile of v1, /device:TPU:1, one launch (start us, length us, event | category | flops | bytes accessed | tf_op | source)
XLA Modules:
  0.0 128.1 jit_solution(12745877944523249263)
XLA Ops:
  0.0 124.5 %updates.1.deltas = f32[4,2,128,128]{3,2,1,0:T(8,128)} custom-call(bf16[440,4096]{1,0:T(8,128)(2,1)} %bitcast.6, f32[147,4096]{1,0:T(8,128)} %bitcast.4, s32[1,4096]{1,0:T(1,128)} %bitcast.7, f32[4,128,512]{2,1,0:T(8,128)} %inv.1, s32[32]{0:T(128)} %order.3, s32[32]{0:T(128)} %block_starts.3), custom_call_target="tpu_custom_call" | custom-call | tf_op jit(solution)/shard_map/updates/pallas_call | solution.py:454
  124.5 3.6 %add_deltas.1 = f32[147,4096]{1,0:T(8,128)} custom-call(f32[147,4096]{1,0:T(8,128)} %bitcast.5, f32[4,2,128,128]{3,2,1,0:T(8,128)} %updates.1.deltas, s32[32]{0:T(128)} %order.3, s32[32]{0:T(128)} %block_starts.3), custom_call_target="tpu_custom_call" | custom-call | tf_op jit(solution)/shard_map/add_deltas/pallas_call | solution.py:508

commit v2 on v1

--- a/solution.py
+++ b/solution.py
@@ -375,12 +375,12 @@
     forward_members(0, 1, MEM, SIB)
     loads[2].wait()
     drain(a.at[pl.ds(0, 1), :, 1 - c], recv.at[SIB])
-    panel(0, 0, whole // 2)
+    panel(0, 0, whole)
+    send_products(0, 1, SP)
     forward_members(1, 3, MEM_REST, SIB_REST)
-    panel(0, whole // 2, whole)
-    send_products(0, 1, SP)
+    drain(iv.at[1 - c], recv.at[INV])
+    split_inverse(1)
     drain(fb.at[1 - c], recv.at[FB])
-    drain(iv.at[1 - c], recv.at[INV])
     drain(o.at[:, 1 - c], recv.at[TERM])
     drain(a.at[pl.ds(1, 3), :, 1 - c], recv.at[SIB_REST])
     split_inverse(0)
@@ -398,7 +398,6 @@
     send_correction(0, None)
     sums_of_products(1, 2, SPR)
     next_residual(0)
-    split_inverse(1)
     partial_delta(1)
     margin(0, 2)
     margin(0, 3)

time: 128 us -> 127 us (level)
  Pallas kernels: 128 us -> 126 us
    pallas_call x1, Pallas kernels: 124 us -> 123 us  [deltas_of(): pl.pallas_call(main_kernel, out_shape=jax.ShapeDtypeStruct((UPD, 2, SPAN,...]
where the time goes in v2:
time: 127 us; the launch traced here: 126 us
  Pallas kernels  126 us (99%)
    pallas_call x1, Pallas kernels, deltas_of(): pl.pallas_call(main_kernel, out_shape=jax.ShapeDtypeStruct((UPD, 2, SPAN,...  123 us
    pallas_call x1, Pallas kernels, add_deltas(): pl.pallas_call(add_kernel, out_shape=jax.ShapeDtypeStruct(wt.shape, wt.dt...  3.64 us

profile of v2, /device:TPU:1, one launch (start us, length us, event | category | flops | bytes accessed | tf_op | source)
XLA Modules:
  0.0 126.5 jit_solution(1784463357068246455)
XLA Ops:
  0.0 122.8 %updates.1.deltas = f32[4,2,128,128]{3,2,1,0:T(8,128)} custom-call(bf16[440,4096]{1,0:T(8,128)(2,1)} %bitcast.6, f32[147,4096]{1,0:T(8,128)} %bitcast.4, s32[1,4096]{1,0:T(1,128)} %bitcast.7, f32[4,128,512]{2,1,0:T(8,128)} %inv.1, s32[32]{0:T(128)} %order.3, s32[32]{0:T(128)} %block_starts.3), custom_call_target="tpu_custom_call" | custom-call | tf_op jit(solution)/shard_map/updates/pallas_call | solution.py:453
  122.8 3.6 %add_deltas.1 = f32[147,4096]{1,0:T(8,128)} custom-call(f32[147,4096]{1,0:T(8,128)} %bitcast.5, f32[4,2,128,128]{3,2,1,0:T(8,128)} %updates.1.deltas, s32[32]{0:T(128)} %order.3, s32[32]{0:T(128)} %block_starts.3), custom_call_target="tpu_custom_call" | custom-call | tf_op jit(solution)/shard_map/add_deltas/pallas_call | solution.py:507

commit v3 on v2

--- a/solution.py
+++ b/solution.py
@@ -119,21 +119,14 @@
 
     def greet_plane(offset):
         row, col, _ = peer(offset)
-        for core in range(2):
-
-            @pl.when((offset > 0) | (core != c))
-            def _():
-                pl.semaphore_signal(
-                    barrier, inc=1, device_id=(row, col, core, z), device_id_type=MESH
-                )
+        pl.semaphore_signal(barrier, inc=1, device_id=(row, col, c, z), device_id_type=MESH)
 
     def greet_column(offset):
-        for core in range(2):
-            pl.semaphore_signal(
-                barrier, inc=1, device_id=(y, x, core, lax.rem(z + offset, COLS)), device_id_type=MESH
-            )
-
-    over(0, CHIPS, greet_plane)
+        other = lax.rem(z + offset, COLS)
+        pl.semaphore_signal(barrier, inc=1, device_id=(y, x, c, other), device_id_type=MESH)
+
+    pl.semaphore_signal(barrier, inc=1, device_id=sib, device_id_type=MESH)
+    over(1, CHIPS, greet_plane)
     over(1, COLS, greet_column)
 
     starts = []
@@ -161,7 +154,7 @@
     for t in range(UPD):
         mem[t] = chosen[t * PIECE : (t + 1) * PIECE]
 
-    pl.semaphore_wait(barrier, 31 + 14)
+    pl.semaphore_wait(barrier, 1 + 15 + 7)
 
     def send_members(first, count, number):
         def body(offset):

time: 127 us -> 127 us (level)
  no operation moved by 1% of the time
where the time goes in v3:
time: 127 us; the launch traced here: 126 us
  Pallas kernels  126 us (99%)
    pallas_call x1, Pallas kernels, deltas_of(): pl.pallas_call(main_kernel, out_shape=jax.ShapeDtypeStruct((UPD, 2, SPAN,...  123 us
    pallas_call x1, Pallas kernels, add_deltas(): pl.pallas_call(add_kernel, out_shape=jax.ShapeDtypeStruct(wt.shape, wt.dt...  3.64 us

profile of v3, /device:TPU:1, one launch (start us, length us, event | category | flops | bytes accessed | tf_op | source)
XLA Modules:
  0.0 126.3 jit_solution(1817977371508720080)
XLA Ops:
  0.0 122.7 %updates.1.deltas = f32[4,2,128,128]{3,2,1,0:T(8,128)} custom-call(bf16[440,4096]{1,0:T(8,128)(2,1)} %bitcast.6, f32[147,4096]{1,0:T(8,128)} %bitcast.4, s32[1,4096]{1,0:T(1,128)} %bitcast.7, f32[4,128,512]{2,1,0:T(8,128)} %inv.1, s32[32]{0:T(128)} %order.3, s32[32]{0:T(128)} %block_starts.3), custom_call_target="tpu_custom_call" | custom-call | tf_op jit(solution)/shard_map/updates/pallas_call | solution.py:446
  122.7 3.6 %add_deltas.1 = f32[147,4096]{1,0:T(8,128)} custom-call(f32[147,4096]{1,0:T(8,128)} %bitcast.5, f32[4,2,128,128]{3,2,1,0:T(8,128)} %updates.1.deltas, s32[32]{0:T(128)} %order.3, s32[32]{0:T(128)} %block_starts.3), custom_call_target="tpu_custom_call" | custom-call | tf_op jit(solution)/shard_map/add_deltas/pallas_call | solution.py:500
